TPU v7x, 32 devices: a whole 2x2x4 slice. The times are simulated.
32 devices in a mesh: row: 4 (over x, core), col: 8 (over z, y).
Axes of the slice: x: 2, y: 2, z: 4, core: 2. Of those that a mesh axis runs over, the one named last changes fastest.
Arguments:
- hamiltonian: float32 [8, 128, 1024], P(None, 'row', 'col'), may hold values from -73 to 73, as said below
Outputs:
- reduced: float32 [8, 128, 1024], P(None, 'row', 'col')
Inputs may be any that keep to these rules, and one draw needn't show every extreme that they name: `hamiltonian`: the matrix A0 is symmetric.
All inputs are finite; a program needn't handle non-finite values.
Results may differ from a plain program's by a relative error of at most 0.0003.
Values sent between devices are 32-bit elements; how exact they have to be, the bound alone decides.
A program may use at most 64 MiB of HBM per device.

v0:
```python
import jax
import jax.numpy as jnp
from jax import lax
from jax.sharding import PartitionSpec as P

B = 256


HIGH = lax.Precision.HIGHEST


def from_root(block, axis, source):
    block = jnp.where(lax.axis_index(axis) == source, block, jnp.zeros_like(block))
    return lax.psum(block, axis)


def flat_rows(blocked):
    return blocked.reshape(-1, blocked.shape[-1])


def transposed_product(left_rows, right_rows):
    return jnp.dot(left_rows.T, right_rows, precision=HIGH, preferred_element_type=jnp.float32)


def outer_blocks(blocked, column_rows):
    return jnp.einsum("ajp,kp->ajk", blocked, column_rows, precision=HIGH)


def local(hamiltonian):
    blocks, strip, columns = hamiltonian.shape
    col_index = lax.axis_index("col")
    owners_each = B // columns
    matrix = hamiltonian
    first_portions = []
    for owner_step in range(2 * owners_each):
        first_portions.append(from_root(hamiltonian, "col", owner_step))
    early_panels = jnp.concatenate(first_portions, axis=2)
    next_panel = early_panels[:, :, B : 2 * B]
    for panel_index in range(2):
        if panel_index == 0:
            panel_blocks = early_panels[:, :, 0:B]
        else:
            panel_blocks = next_panel
        panel_rows = flat_rows(panel_blocks)
        gram_matrix = lax.psum(transposed_product(panel_rows, panel_rows), "row")
        factor = jnp.linalg.cholesky(gram_matrix)
        reflector = lax.linalg.triangular_solve(
            factor, panel_rows, left_side=False, lower=True, transpose_a=True
        )
        reflector_blocks = reflector.reshape(blocks, strip, B)
        partial_image = transposed_product(flat_rows(matrix), reflector)
        image_piece = lax.psum_scatter(partial_image, "row", scatter_dimension=0, tiled=True)
        own_reflector = lax.dynamic_index_in_dim(reflector_blocks, col_index, 0, keepdims=False)
        reflector_cols, shared_cols = (
            lax.all_gather(own_reflector, "row", axis=0, tiled=True),
            lax.all_gather(image_piece, "row", axis=0, tiled=True),
        )
        product_own = None
        image_rows = lax.all_gather(image_piece[None], "col", axis=0, tiled=True)
        corner = lax.psum(transposed_product(reflector, flat_rows(image_rows)), "row")
        corrected = 2.0 * image_rows - 2.0 * jnp.einsum(
            "ajp,pq->ajq", reflector_blocks, corner, precision=HIGH
        )
        corrected_cols = 2.0 * shared_cols - 2.0 * jnp.dot(
            reflector_cols, corner, precision=HIGH, preferred_element_type=jnp.float32
        )
        matrix = (
            matrix
            - outer_blocks(reflector_blocks, corrected_cols)
            - outer_blocks(corrected, reflector_cols)
        )
        product_own = corrected
        if panel_index == 0:
            basis_next = reflector_blocks[owners_each : 2 * owners_each]
            product_next = product_own[owners_each : 2 * owners_each]
            basis_gathered, product_gathered = (
                lax.all_gather(basis_next, "row", axis=1, tiled=True),
                lax.all_gather(product_next, "row", axis=1, tiled=True),
            )
            next_panel = (
                next_panel
                - outer_blocks(reflector_blocks, flat_rows(product_gathered))
                - outer_blocks(product_own, flat_rows(basis_gathered))
            )
    return matrix


def solution(mesh):
    placed = (P(None, "row", "col"),)
    return jax.shard_map(
        local, mesh=mesh, in_specs=placed, out_specs=P(None, "row", "col"), check_vma=False
    )
```

profile of v0, /device:TPU:0, one launch (start us, length us, event | category | flops | bytes accessed | tf_op | source)
XLA Modules:
  0.0 470.8 jit_solution(11909027406764640253)
XLA Ops:
  6.5 1.7 broadcast_select_fusion.1
  8.3 78.8 %all-reduce.16.cloned.1.call-done = (f32[8,32,128]{2,1,0:T(8,128)}, f32[8,32,128]{2,1,0:T(8,128)}, f32[8,32,128]{2,1,0:T(8,128)}, f32[8,32,128]{2,1,0:T(8,128)}) async-done(((f32[8,32,128]{2,1,0:T(8,128)}, f32[8,32,128]{2,1,0:T(8,128)}, f32[8,32,128]{2,1,0:T(8,128)}, f32[8,32,128]{2,1,0:T(8,128)}), (f32[8,32,128]{2,1,0:T(8,128)}, f32[8,32,128]{2,1,0:T(8,128)}, f32[8,32,128]{2,1,0:T(8,128)}, ...) | async-done | bytes 524304 | tf_op jit(solution)/shard_map/psum | solution.py:14
  87.1 0.9 constant_dynamic-update-slice_fusion.1
  88.1 1.3 convolution_bitcast_fusion.1
  89.4 31.6 %all-reduce.8.cloned.1.call-done = f32[256,256]{0,1:T(8,128)} async-done(((f32[256,256]{0,1:T(8,128)}), f32[256,256]{0,1:T(8,128)}) %all-reduce.8.cloned.1.call-update) | async-done | bytes 262160 | tf_op jit(solution)/shard_map/psum | solution.py:45
  121.0 1.1 copy.31
  122.2 11.7 %cholesky.130 = f32[128,128]{1,0:T(8,128)S(1)} custom-call(f32[128,128]{1,0:T(8,128)S(1)} %cholesky.194), custom_call_target="Cholesky" | custom-call | tf_op jit(solution)/shard_map/jit(cholesky)/cholesky | solution.py:46
  134.0 9.8 %custom-call.13 = f32[1,128,128]{1,2,0:T(8,128)S(1)} custom-call(f32[1,128,128]{2,1,0:T(8,128)S(1)} %get-tuple-element.58), custom_call_target="InvertDiagBlocksLowerTriangular" | custom-call | tf_op jit(solution)/shard_map/jit(cholesky)/cholesky | solution.py:46
  144.3 11.7 %cholesky.147 = f32[128,128]{1,0:T(8,128)S(1)} custom-call(f32[128,128]{1,0:T(8,128)S(1)} %convolution_subtract_fusion.9), custom_call_target="Cholesky" | custom-call | tf_op jit(solution)/shard_map/jit(cholesky)/cholesky | solution.py:46
  156.1 0.6 compare_reduce_fusion.2
  158.0 4.0 while.4
  158.8 1.3 bitcast_dynamic-update-slice_fusion.4
  160.7 1.3 bitcast_dynamic-update-slice_fusion.4
  162.0 19.7 %custom-call.14 = f32[2,128,128]{1,2,0:T(8,128)S(1)} custom-call(f32[2,128,128]{2,1,0:T(8,128)S(1)} %get-tuple-element.21), custom_call_target="InvertDiagBlocksLowerTriangular" | custom-call | tf_op jit(solution)/shard_map/triangular_solve/custom-call.0 | solution.py:47
  182.8 0.9 copy-done
  184.0 0.8 copy.47
  185.2 5.4 %all-gather = f32[1,128,256]{2,1,0:T(8,128)S(1)} all-gather(f32[1,32,256]{2,1,0:T(8,128)S(1)} %constant_dynamic-slice_fusion.3), channel_id=2, replica_groups=mesh['row'=4,'col'=8] {'row'}, dimensions={1}, use_global_device_ids=true | all-gather | bytes 163840 | tf_op jit(solution)/shard_map/all_gather | solution.py:55
  190.6 5.8 %all_gather.28 = f32[2,128,256]{2,1,0:T(8,128)S(1)} all-gather(f32[2,32,256]{2,1,0:T(8,128)S(1)} %bitcast.155), channel_id=1, replica_groups=mesh['row'=4,'col'=8] {'row'}, dimensions={1}, use_global_device_ids=true | all-gather | bytes 327680 | tf_op jit(solution)/shard_map/all_gather | solution.py:77
  196.4 8.1 %reduce-scatter.7.cloned.1.call-done = f32[32,256]{1,0:T(8,128)} async-done(((f32[128,256]{1,0:T(8,128)}), f32[32,256]{1,0:T(8,128)}) %reduce-scatter.7.cloned.1.call-update) | async-done | bytes 32784 | tf_op jit(solution)/shard_map/reduce_scatter | solution.py:52
  204.6 31.0 %all-gather.1 = f32[256,256]{1,0:T(8,128)S(1)} all-gather(f32[32,256]{1,0:T(8,128)} %reduce-scatter.7.cloned.1.call-done), channel_id=3, replica_groups=mesh['row'=4,'col'=8] {'col'}, dimensions={0}, use_global_device_ids=true | all-gather | bytes 294912 | tf_op jit(solution)/shard_map/all_gather | solution.py:59
  235.6 1.1 fusion.31
  236.8 0.7 copy-done.5
  237.4 5.4 %all_gather.24 = f32[128,256]{1,0:T(8,128)S(1)} all-gather(f32[32,256]{1,0:T(8,128)S(1)} %copy-done.5), channel_id=1, replica_groups=mesh['row'=4,'col'=8] {'row'}, dimensions={0}, use_global_device_ids=true | all-gather | bytes 163840 | tf_op jit(solution)/shard_map/all_gather | solution.py:56
  242.8 26.2 %all-reduce.10.cloned.1.call-done = f32[256,256]{1,0:T(8,128)} async-done(((f32[256,256]{1,0:T(8,128)}), f32[256,256]{1,0:T(8,128)}) %all-reduce.10.cloned.1.call-update) | async-done | bytes 262160 | tf_op jit(solution)/shard_map/psum | solution.py:60
  269.1 1.2 fusion.5
  271.7 5.9 %all_gather.27 = f32[2,128,256]{2,1,0:T(8,128)S(1)} all-gather(f32[2,32,256]{2,1,0:T(8,128)S(1)} %slice.87), channel_id=1, replica_groups=mesh['row'=4,'col'=8] {'row'}, dimensions={1}, use_global_device_ids=true | all-gather | bytes 327680 | tf_op jit(solution)/shard_map/all_gather | solution.py:78
  278.4 1.3 convolution_bitcast_fusion
  280.4 31.8 %all-reduce.12.cloned.1.call-done = f32[256,256]{0,1:T(8,128)} async-done(((f32[256,256]{0,1:T(8,128)}), f32[256,256]{0,1:T(8,128)}) %all-reduce.12.cloned.1.call-update) | async-done | bytes 262160 | tf_op jit(solution)/shard_map/psum | solution.py:45
  312.2 1.1 copy.37
  313.4 11.7 %cholesky.164 = f32[128,128]{1,0:T(8,128)S(1)} custom-call(f32[128,128]{1,0:T(8,128)S(1)} %cholesky.197), custom_call_target="Cholesky" | custom-call | tf_op jit(solution)/shard_map/jit(cholesky)/cholesky | solution.py:46
  325.2 9.8 %custom-call.15 = f32[1,128,128]{1,2,0:T(8,128)S(1)} custom-call(f32[1,128,128]{2,1,0:T(8,128)S(1)} %get-tuple-element.54), custom_call_target="InvertDiagBlocksLowerTriangular" | custom-call | tf_op jit(solution)/shard_map/jit(cholesky)/cholesky | solution.py:46
  335.5 11.7 %cholesky.181 = f32[128,128]{1,0:T(8,128)S(1)} custom-call(f32[128,128]{1,0:T(8,128)S(1)} %convolution_subtract_fusion.8), custom_call_target="Cholesky" | custom-call | tf_op jit(solution)/shard_map/jit(cholesky)/cholesky | solution.py:46
  347.2 0.6 compare_reduce_fusion.1
  347.9 0.6 compare_reduce_fusion
  349.8 4.1 while.5
  350.6 1.3 bitcast_dynamic-update-slice_fusion.5
  352.5 1.3 bitcast_dynamic-update-slice_fusion.5
  353.8 19.7 %custom-call.16 = f32[2,128,128]{1,2,0:T(8,128)S(1)} custom-call(f32[2,128,128]{2,1,0:T(8,128)S(1)} %get-tuple-element.22), custom_call_target="InvertDiagBlocksLowerTriangular" | custom-call | tf_op jit(solution)/shard_map/triangular_solve/custom-call.0 | solution.py:47
  374.6 1.0 fusion.30
  375.9 5.4 %all-gather.2 = f32[1,128,256]{2,1,0:T(8,128)S(1)} all-gather(f32[1,32,256]{2,1,0:T(8,128)S(1)} %constant_dynamic-slice_fusion.2), channel_id=4, replica_groups=mesh['row'=4,'col'=8] {'row'}, dimensions={1}, use_global_device_ids=true | all-gather | bytes 163840 | tf_op jit(solution)/shard_map/all_gather | solution.py:55
  381.3 14.1 %reduce-scatter.9.cloned.1.call-done = f32[32,256]{1,0:T(8,128)} async-done(((f32[128,256]{1,0:T(8,128)}), f32[32,256]{1,0:T(8,128)}) %reduce-scatter.9.cloned.1.call-update) | async-done | bytes 32784 | tf_op jit(solution)/shard_map/reduce_scatter | solution.py:52
  395.4 31.0 %all-gather.3 = f32[256,256]{1,0:T(8,128)S(1)} all-gather(f32[32,256]{1,0:T(8,128)} %reduce-scatter.9.cloned.1.call-done), channel_id=5, replica_groups=mesh['row'=4,'col'=8] {'col'}, dimensions={0}, use_global_device_ids=true | all-gather | bytes 294912 | tf_op jit(solution)/shard_map/all_gather | solution.py:59
  426.4 1.1 fusion.29
  427.6 0.7 copy-done.6
  428.3 5.4 %all_gather.29 = f32[128,256]{1,0:T(8,128)S(1)} all-gather(f32[32,256]{1,0:T(8,128)S(1)} %copy-done.6), channel_id=1, replica_groups=mesh['row'=4,'col'=8] {'row'}, dimensions={0}, use_global_device_ids=true | all-gather | bytes 163840 | tf_op jit(solution)/shard_map/all_gather | solution.py:56
  433.7 26.2 %all-reduce.14.cloned.1.call-done = f32[256,256]{1,0:T(8,128)} async-done(((f32[256,256]{1,0:T(8,128)}), f32[256,256]{1,0:T(8,128)}) %all-reduce.14.cloned.1.call-update) | async-done | bytes 262160 | tf_op jit(solution)/shard_map/psum | solution.py:60
  459.9 1.2 fusion.3
  462.5 1.0 convolution_subtract_fusion.2
  (85 shorter events, 11.1 us)
Async XLA Ops:
  6.5 80.5 %all-reduce.16.cloned.1.call-start = ((), (), s32[]{:S(2)}) async-start(), calls=%async_computation.8 | async-start | bytes 1048576 | tf_op jit(solution)/shard_map/psum | solution.py:14
  8.3 112.7 %all-reduce.8.cloned.1.call-start = ((), (), s32[]{:S(2)}) async-start(), calls=%async_computation.2 | async-start | bytes 524288 | tf_op jit(solution)/shard_map/psum | solution.py:45
  87.1 1.0 copy-start.7
  89.4 115.2 %reduce-scatter.7.cloned.1.call-start = ((), (), s32[]{:S(2)}) async-start(), calls=%async_computation.6 | async-start | bytes 163840 | tf_op jit(solution)/shard_map/reduce_scatter | solution.py:52
  121.0 1.2 copy-start.1
  182.7 0.9 copy-start
  184.8 84.3 %all-reduce.10.cloned.1.call-start = ((), (), s32[]{:S(2)}) async-start(), calls=%async_computation.3 | async-start | bytes 524288 | tf_op jit(solution)/shard_map/psum | solution.py:60
  236.7 0.8 copy-start.5
  236.7 75.5 %all-reduce.12.cloned.1.call-start = ((), (), s32[]{:S(2)}) async-start(), calls=%async_computation.4 | async-start | bytes 524288 | tf_op jit(solution)/shard_map/psum | solution.py:45
  270.3 1.0 copy-start.3
  271.6 5.9 %copy-start.8 = (f32[8,32,128]{2,1,0:T(8,128)S(1)}, f32[8,32,128]{2,1,0:T(8,128)}, u32[]{:S(2)}) copy-start(f32[8,32,128]{2,1,0:T(8,128)} %get-tuple-element.41) | copy-start | bytes 393220
  271.7 5.9 %copy-start.9 = (f32[8,32,128]{2,1,0:T(8,128)S(1)}, f32[8,32,128]{2,1,0:T(8,128)}, u32[]{:S(2)}) copy-start(f32[8,32,128]{2,1,0:T(8,128)} %get-tuple-element.42) | copy-start | bytes 393220
  279.7 115.7 %reduce-scatter.9.cloned.1.call-start = ((), (), s32[]{:S(2)}) async-start(), calls=%async_computation.7 | async-start | bytes 163840 | tf_op jit(solution)/shard_map/reduce_scatter | solution.py:52
  312.2 1.2 copy-start.2
  375.6 84.3 %all-reduce.14.cloned.1.call-start = ((), (), s32[]{:S(2)}) async-start(), calls=%async_computation.5 | async-start | bytes 524288 | tf_op jit(solution)/shard_map/psum | solution.py:60
  427.5 0.8 copy-start.6
  461.1 1.0 copy-start.4
Sparse Core Ops, SparseCore 0:
  11.1 75.9 all-reduce.15
  89.5 31.4 all-reduce.7
  184.9 19.6 reduce-scatter.6
  236.8 32.2 all-reduce.9
  279.9 32.2 all-reduce.11
  375.8 19.6 reduce-scatter.8
  427.6 32.1 all-reduce.13
where the time goes:
time: 479 us; the launch traced here: 471 us
  waiting for transfers between devices  217 us (45%)
  other arithmetic  110 us (23%)
  blocking collectives  95.4 us (20%)
  between operations  16.8 us (4%)
  local copies, waits for them, and re-layouts  15.5 us (3%)
  matrix products  15.3 us (3%)
    psum x1, waiting for transfers between devices, from_root(): return lax.psum(block, axis)  78.8 us
    another operation x13, other arithmetic, local(): factor = jnp.linalg.cholesky(gram_matrix)  68.5 us
    psum x2, waiting for transfers between devices, local(): gram_matrix = lax.psum(transposed_product(panel_rows, panel_rows), 'row')  63.3 us
    all_gather x2, blocking collectives, local(): image_rows = lax.all_gather(image_piece[None], 'col', axis=0, tiled=True)  62 us
    psum x2, waiting for transfers between devices, local(): lax.psum(transposed_product(reflector, flat_rows(image_rows)), 'row')  52.4 us
    another operation x8, other arithmetic, local(): lax.linalg.triangular_solve(factor, panel_rows, left_side=False, lower=Tr...  39.5 us
    reduce_scatter x2, waiting for transfers between devices, local(): lax.psum_scatter(partial_image, 'row', scatter_dimension=0, tiled=True)  22.2 us
    all_gather x2, blocking collectives, local(): lax.all_gather(own_reflector, 'row', axis=0, tiled=True)  10.8 us
  transfers between devices with their start and end apart: 7, of which 7 were waited for; matrix products, arithmetic and copies ran while one was open for 0% of the time, Pallas kernels for 0%

commit v1 on v0

--- a/solution.py
+++ b/solution.py
@@ -1,12 +1,78 @@
 import jax
 import jax.numpy as jnp
 from jax import lax
+from jax.experimental import pallas as pl
+from jax.experimental.pallas import tpu as pltpu
 from jax.sharding import PartitionSpec as P
 
 B = 256
-
-
-HIGH = lax.Precision.HIGHEST
+NB = 32
+LANES = 128
+REPLICATED_BYTES = 1 << 25
+HIGHEST = lax.Precision.HIGHEST
+
+
+def dot(left, right, dims, precision=HIGHEST):
+    return lax.dot_general(
+        left, right, (dims, ((), ())), precision=precision, preferred_element_type=jnp.float32
+    )
+
+
+def nn(left, right, precision=HIGHEST):
+    return dot(left, right, ((1,), (0,)), precision)
+
+
+def nt(left, right, precision=HIGHEST):
+    return dot(left, right, ((1,), (1,)), precision)
+
+
+def tn(left, right, precision=HIGHEST):
+    return dot(left, right, ((0,), (0,)), precision)
+
+
+def inverse_factor_kernel(gram_ref, out_ref, work_ref):
+    size = gram_ref.shape[0]
+    work_ref[:, :size] = gram_ref[...]
+    work_ref[:, size:] = (
+        lax.broadcasted_iota(jnp.int32, (size, size), 0)
+        == lax.broadcasted_iota(jnp.int32, (size, size), 1)
+    ).astype(jnp.float32)
+    row_ids = lax.broadcasted_iota(jnp.int32, (NB, 1), 0)
+    for low in range(0, size, NB):
+        high = low + NB
+        first = low // LANES * LANES
+        last = size + -(-high // LANES) * LANES
+        rows = work_ref[low:high, first:last]
+        pivots = jnp.ones((NB, 1), jnp.float32)
+        for j in range(NB):
+            lane = low + j - first
+            column = rows[:, lane : lane + 1]
+            pivot = column[j : j + 1]
+            pivots = jnp.where(row_ids == j, pivot, pivots)
+            if j < NB - 1:
+                below = jnp.where(row_ids > j, column, 0.0)
+                rows = rows - below * (rows[j : j + 1] * (1.0 / pivot))
+        rows = rows * lax.rsqrt(pivots)
+        out_ref[low:high, :] = jnp.zeros((NB, size), jnp.float32)
+        out_ref[low:high, : last - size] = rows[:, size - first :]
+        if high < size:
+            trailing = rows[:, high // LANES * LANES - first : size - first].T
+            trailing = trailing[high % LANES :]
+            work_ref[high:, first:last] -= nn(trailing, rows, HIGHEST)
+
+
+def inverse_factor(gram):
+    size = gram.shape[0]
+    return pl.pallas_call(
+        inverse_factor_kernel,
+        out_shape=jax.ShapeDtypeStruct(gram.shape, jnp.float32),
+        in_specs=[pl.BlockSpec(memory_space=pltpu.VMEM)],
+        out_specs=pl.BlockSpec(memory_space=pltpu.VMEM),
+        scratch_shapes=[pltpu.VMEM((size, 2 * size), jnp.float32)],
+        cost_estimate=pl.CostEstimate(
+            flops=4 * size**3 * 64, bytes_accessed=8 * size * size, transcendentals=size
+        ),
+    )(gram)
 
 
 def from_root(block, axis, source):
@@ -19,14 +85,14 @@
 
 
 def transposed_product(left_rows, right_rows):
-    return jnp.dot(left_rows.T, right_rows, precision=HIGH, preferred_element_type=jnp.float32)
+    return jnp.dot(left_rows.T, right_rows, precision=HIGHEST, preferred_element_type=jnp.float32)
 
 
 def outer_blocks(blocked, column_rows):
-    return jnp.einsum("ajp,kp->ajk", blocked, column_rows, precision=HIGH)
-
-
-def local(hamiltonian):
+    return jnp.einsum("ajp,kp->ajk", blocked, column_rows, precision=HIGHEST)
+
+
+def local_shared(hamiltonian):
     blocks, strip, columns = hamiltonian.shape
     col_index = lax.axis_index("col")
     owners_each = B // columns
@@ -59,10 +125,10 @@
         image_rows = lax.all_gather(image_piece[None], "col", axis=0, tiled=True)
         corner = lax.psum(transposed_product(reflector, flat_rows(image_rows)), "row")
         corrected = 2.0 * image_rows - 2.0 * jnp.einsum(
-            "ajp,pq->ajq", reflector_blocks, corner, precision=HIGH
+            "ajp,pq->ajq", reflector_blocks, corner, precision=HIGHEST
         )
         corrected_cols = 2.0 * shared_cols - 2.0 * jnp.dot(
-            reflector_cols, corner, precision=HIGH, preferred_element_type=jnp.float32
+            reflector_cols, corner, precision=HIGHEST, preferred_element_type=jnp.float32
         )
         matrix = (
             matrix
@@ -85,6 +151,72 @@
     return matrix
 
 
+def local(hamiltonian):
+    blocks, strip, columns = hamiltonian.shape
+    if 8 * 4 * B * blocks * strip * lax.axis_size("row") > REPLICATED_BYTES:
+        return local_shared(hamiltonian)
+    row_index = lax.axis_index("row")
+    col_index = lax.axis_index("col")
+    width = strip * lax.axis_size("row")
+    order = blocks * width
+    each = B // width
+
+    def panel_rows(index):
+        part = hamiltonian[index * each : (index + 1) * each]
+        part = lax.all_gather(part, ("row", "col"), axis=0)
+        part = part.reshape(lax.axis_size("row"), lax.axis_size("col"), each, strip, columns)
+        return part.transpose(2, 0, 3, 1, 4).reshape(B, order)
+
+    def spread(piece):
+        whole = lax.all_gather(piece, "col", axis=0)
+        return whole.transpose(1, 0, 2).reshape(B, order)
+
+    def own_columns(whole):
+        return lax.dynamic_slice_in_dim(whole, col_index * columns, columns, 1)
+
+    def own_rows(whole):
+        whole = whole.reshape(B, blocks, width)
+        mine = lax.dynamic_slice_in_dim(whole, row_index * strip, strip, 2)
+        return mine.reshape(B, blocks * strip)
+
+    panel = panel_rows(0)
+    strip_cols = lax.all_gather(hamiltonian, "row", axis=1, tiled=True).reshape(order, columns)
+    later = panel_rows(1)
+
+    image = spread(nn(panel, strip_cols, HIGHEST))
+    inverse = inverse_factor(nt(panel, panel, HIGHEST))
+    basis = nn(inverse, panel)
+    image = nn(inverse, image)
+    corner = nt(basis, image)
+    product = 2.0 * image - 2.0 * tn(corner, basis)
+
+    later = (
+        later
+        - tn(product[:, B : 2 * B], basis)
+        - tn(basis[:, B : 2 * B], product)
+    )
+    image2 = spread(nn(later, strip_cols, HIGHEST))
+    inverse2 = inverse_factor(nt(later, later, HIGHEST))
+    with_product = nt(later, product)
+    with_basis = nt(later, basis)
+    inner = nt(later, image2)
+    inner = inner - nt(with_basis, with_product) - nt(with_product, with_basis)
+    corner2 = nt(nn(inverse2, inner), inverse2)
+
+    def second(pick):
+        own_basis, own_product = pick(basis), pick(product)
+        basis2 = nn(inverse2, pick(later))
+        moved = pick(image2) - nn(with_product, own_basis) - nn(with_basis, own_product)
+        product2 = 2.0 * nn(inverse2, moved) - 2.0 * tn(corner2, basis2)
+        return own_basis, own_product, basis2, product2
+
+    row_b1, row_p1, row_b2, row_p2 = second(own_rows)
+    col_b1, col_p1, col_b2, col_p2 = second(own_columns)
+    left = jnp.concatenate([row_b1, row_p1, row_b2, row_p2], axis=0)
+    right = jnp.concatenate([col_p1, col_b1, col_p2, col_b2], axis=0)
+    return hamiltonian - tn(left, right).reshape(hamiltonian.shape)
+
+
 def solution(mesh):
     placed = (P(None, "row", "col"),)
     return jax.shard_map(

time: 479 us -> 242 us (0.51); the launches traced: 471 us -> 239 us
  other arithmetic: 110 us -> 0.67 us
  waiting for transfers between devices: 217 us -> 111 us
  blocking collectives: 95.4 us -> 8.65 us
  Pallas kernels: 0 us -> 52.5 us
  matrix products: 15.3 us -> 28.7 us
  local copies, waits for them, and re-layouts: 15.5 us -> 23.3 us
    psum x5 -> x0, waiting for transfers between devices: 195 us -> none  [the longest x1 78.8 us: from_root(): return lax.psum(block, axis)]
    all_gather x0 -> x4, waiting for transfers between devices: none -> 110 us  [the longest x2 101 us: panel_rows(): part = lax.all_gather(part, ('row', 'col'), axis=0)]
    another operation x21 -> x0, other arithmetic: 108 us -> none  [the longest x13 68.5 us: local(): factor = jnp.linalg.cholesky(gram_matrix)]
    all_gather x8 -> x1, blocking collectives: 95.4 us -> 8.65 us  [local(): lax.all_gather(hamiltonian, 'row', axis=1, tiled=True)]
    pallas_call x0 -> x2, Pallas kernels: none -> 52.5 us  [inverse_factor(): pl.pallas_call(inverse_factor_kernel, out_shape=jax.ShapeDtypeStruct(gram...]
    reduce_scatter x2 -> x0, waiting for transfers between devices: 22.2 us -> none  [local(): lax.psum_scatter(partial_image, 'row', scatter_dimension=0, tiled=True)]
    dot_general x15 -> x28, matrix products: 11.3 us -> 28.7 us  [dot(): lax.dot_general(left, right, (dims, ((), ())), precision=precision, prefe...]
    reshape x0 -> x8, local copies, waits for them, and re-layouts: none -> 9.4 us  [the longest x2 4.64 us: panel_rows(): part.reshape(lax.axis_size('row'), lax.axis_size('col'), each, strip, col...]
  transfers between devices with their start and end apart: 7 -> 4, of which waited for: 7 -> 4; matrix products, arithmetic and copies ran while one was open for 0% -> 10% of each run, Pallas kernels for 0% -> 22%
where the time goes in v1:
time: 242 us; the launch traced here: 239 us
  waiting for transfers between devices  111 us (46%)
  Pallas kernels  52.5 us (22%)
  matrix products  28.7 us (12%)
  local copies, waits for them, and re-layouts  23.3 us (10%)
  between operations  13.9 us (6%)
  blocking collectives  8.65 us (4%)
    all_gather x2, waiting for transfers between devices, panel_rows(): part = lax.all_gather(part, ('row', 'col'), axis=0)  101 us
    pallas_call x2, Pallas kernels, inverse_factor(): pl.pallas_call(inverse_factor_kernel, out_shape=jax.ShapeDtypeStruct(gram...  52.5 us
    dot_general x28, matrix products, dot(): lax.dot_general(left, right, (dims, ((), ())), precision=precision, prefe...  28.7 us
    all_gather x2, waiting for transfers between devices, spread(): whole = lax.all_gather(piece, 'col', axis=0)  8.65 us
    all_gather x1, blocking collectives, local(): lax.all_gather(hamiltonian, 'row', axis=1, tiled=True)  8.65 us
    unnamed x39, local copies, waits for them, and re-layouts  5.46 us
  transfers between devices with their start and end apart: 4, of which 4 were waited for; matrix products, arithmetic and copies ran while one was open for 10% of the time, Pallas kernels for 22%

profile of v1, /device:TPU:0, one launch (start us, length us, event | category | flops | bytes accessed | tf_op | source)
XLA Modules:
  0.0 238.9 jit_solution(12513267025870612180)
XLA Ops:
  6.5 1.5 fusion.33
  8.1 0.7 all-gather.13.cloned.1.call-update
  8.8 8.6 %all_gather.29 = f32[8,128,128]{2,1,0:T(8,128)S(1)} all-gather(f32[8,32,128]{2,1,0:T(8,128)S(1)} %copy-done.12), channel_id=1, replica_groups=mesh['row'=4,'col'=8] {'row'}, dimensions={1}, use_global_device_ids=true | all-gather | bytes 655360 | tf_op jit(solution)/shard_map/all_gather | solution.py:183
  17.5 49.4 %all-gather.9.cloned.1.call-done = f32[64,32,128]{2,1,0:T(8,128)} async-done(((f32[2,32,128]{2,1,0:T(8,128)}), f32[64,32,128]{2,1,0:T(8,128)}) %all-gather.9.cloned.1.call-update) | async-done | bytes 1048592 | tf_op jit(solution)/shard_map/all_gather | solution.py:166
  66.9 1.8 copy.13
  68.7 1.7 fusion.3
  70.7 52.0 %all-gather.13.cloned.1.call-done = f32[64,32,128]{2,1,0:T(8,128)} async-done(((f32[2,32,128]{2,1,0:T(8,128)}), f32[64,32,128]{2,1,0:T(8,128)}) %all-gather.13.cloned.1.call-update) | async-done | bytes 1048592 | tf_op jit(solution)/shard_map/all_gather | solution.py:166
  122.7 2.8 %copy.17 = f32[4,8,2,32,128]{4,1,3,0,2:T(8,128)} copy(f32[4,8,2,32,128]{4,3,2,1,0:T(8,128)} %bitcast.100) | data formatting | bytes 2097152 | tf_op jit(solution)/shard_map/reshape | solution.py:167
  125.5 1.9 fusion.7.gram_ref
  127.5 26.2 %shard_map.17 = f32[256,256]{1,0:T(8,128)} custom-call(f32[256,256]{1,0:T(8,128)} %fusion.7.gram_ref), custom_call_target="tpu_custom_call" | custom-call | flops 4294967296 | bytes 524288 | tf_op jit(solution)/shard_map/pallas_call | solution.py:66
  153.6 2.1 fusion.5
  156.1 0.8 copy.22
  156.9 0.7 constant_dynamic-slice_fusion.1
  157.6 6.8 %all-gather.11.cloned.1.call-done = f32[2048,128]{1,0:T(8,128)} async-done(((f32[256,128]{1,0:T(8,128)}), f32[2048,128]{1,0:T(8,128)}) %all-gather.11.cloned.1.call-update) | async-done | bytes 1048592 | tf_op jit(solution)/shard_map/all_gather | solution.py:171
  164.4 1.6 copy.15
  166.0 1.0 fusion.34
  167.1 1.0 fusion.35
  168.1 1.3 fusion
  169.5 1.3 copy.26
  170.8 1.2 convolution_subtract_fusion.1
  172.0 1.0 convolution_subtract_fusion
  173.0 1.6 fusion.38
  174.7 1.3 copy.27
  176.0 1.8 constant_dynamic-slice_fusion.4
  177.8 0.8 copy.23
  178.7 0.7 constant_dynamic-slice_fusion.2
  179.3 1.8 fusion.36.gram_ref
  181.1 26.4 %shard_map.18 = f32[256,256]{1,0:T(8,128)} custom-call(f32[256,256]{1,0:T(8,128)} %fusion.36.gram_ref), custom_call_target="tpu_custom_call" | custom-call | flops 4294967296 | bytes 524288 | tf_op jit(solution)/shard_map/pallas_call | solution.py:66
  207.5 2.0 fusion.29
  209.5 1.2 fusion.37
  210.7 1.8 fusion.40
  212.5 1.0 fusion.39
  213.5 1.9 all-gather.15.cloned.1.call-done
  215.4 1.6 copy.19
  216.9 0.7 constant_dynamic-slice_fusion
  217.6 1.0 fusion.41
  218.7 0.9 copy-done.16
  219.6 0.9 copy-done.1
  220.9 0.4 convolution_subtract_fusion.2
  221.5 0.8 copy-done.6
  222.7 0.5 copy-done.14
  223.6 0.5 copy-done.15
  225.7 0.5 copy-done.8
  227.0 0.6 copy-done.10
  227.6 0.6 fusion.1
  228.5 0.6 fusion.2
  229.5 1.8 fusion.9
  231.3 0.7 sub.47
  (52 shorter events, 5.3 us)
Async XLA Ops:
  6.5 2.3 copy-start.12
  6.5 60.4 %all-gather.9.cloned.1.call-start = ((), (), s32[]{:S(2)}) async-start(), calls=%async_computation | async-start | bytes 1081344 | tf_op jit(solution)/shard_map/all_gather | solution.py:166
  8.0 114.7 %all-gather.13.cloned.1.call-start = ((), (), s32[]{:S(2)}) async-start(), calls=%async_computation.2 | async-start | bytes 1081344 | tf_op jit(solution)/shard_map/all_gather | solution.py:166
  8.8 155.6 %all-gather.11.cloned.1.call-start = ((), (), s32[]{:S(2)}) async-start(), calls=%async_computation.1 | async-start | bytes 1179648 | tf_op jit(solution)/shard_map/all_gather | solution.py:171
  17.5 51.2 %copy-start.2 = (f32[8,128,128]{2,1,0:T(8,128)}, f32[8,128,128]{2,1,0:T(8,128)S(1)}, u32[]{:S(2)}) copy-start(f32[8,128,128]{2,1,0:T(8,128)S(1)} %all_gather.29) | copy-start | bytes 1572868
  70.5 144.9 %all-gather.15.cloned.1.call-start = ((), (), s32[]{:S(2)}) async-start(), calls=%async_computation.3 | async-start | bytes 1179648 | tf_op jit(solution)/shard_map/all_gather | solution.py:171
  156.1 0.8 copy-start.5
  164.4 1.6 copy-start.9
  169.5 1.3 copy-start.4
  172.0 1.1 copy-start.3
  177.8 0.8 copy-start.7
  207.5 2.1 copy-start
  207.5 2.1 copy-start.11
  218.6 0.9 copy-start.16
  219.5 0.9 copy-start.1
  221.3 1.0 copy-start.6
  222.3 0.9 copy-start.14
  223.2 0.9 copy-start.15
  225.2 1.0 copy-start.8
  226.6 1.0 copy-start.10
  227.6 0.9 copy-start.13
  228.5 0.9 copy-start.17
  228.5 1.0 copy-start.18
Sparse Core Ops, SparseCore 0:
  10.4 56.4 all-gather.8
  70.0 52.7 all-gather.12
  124.9 39.5 all-gather.10
  176.2 39.1 all-gather.14
